TPU v7x, 128 devices: a whole 4x4x4 slice. The times are simulated.
128 devices in a mesh: row: 16 (over z_hi, y, core), col: 8 (over z_lo, x).
Axes of the slice: x: 4, y: 4, z: 4 (z_hi: 2, z_lo: 2; z = z_hi * 2 + z_lo), core: 2. Of those that a mesh axis runs over, the one named last changes fastest.
Arguments:
- grad_out: bfloat16 [262144, 256], P(('row', 'col')), may hold values from -6 to 6
- preact: bfloat16 [262144, 256], P(('row', 'col')), may hold values from -6 to 6
- features: bfloat16 [262144, 256], P(('col', 'row')), may hold values from -6 to 6
- weight: bfloat16 [256, 256], replicated, may hold values from -0.375 to 0.375
- tiles: bfloat16 [16, 8, 320, 128, 128], P('row', 'col'), may hold values from -0.099609375 to 0.099609375
- tile_rows: int32 [16, 8, 320], P('row', 'col'), may hold values from 0 to 127
- tile_cols: int32 [16, 8, 320], P('row', 'col'), may hold values from 0 to 255
- live_counts: int32 [16, 8], P('row', 'col'), may hold values from 80 to 320, as said below
Outputs:
- grad_features: bfloat16 [262144, 256], P(('col', 'row'))
- grad_weight: float32 [256, 256], replicated
Inputs may be any that keep to these rules, and one draw needn't show every extreme that they name: `live_counts`: some block holds exactly 320 live tiles in every draw.
All inputs are finite; a program needn't handle non-finite values.
Results may differ from a plain program's by a relative error of at most 0.02.
Values may be sent and summed in bfloat16 or wider, within the bound.
A program may use at most 192 MiB of HBM per device.

v0:
```python
import math
import jax
import jax.numpy as jnp
from jax import lax
from jax.sharding import PartitionSpec as P


def body(grad_out, preact, features, weight, tiles, tile_rows, tile_cols, live_counts):
    width = grad_out.shape[1]
    masked = jnp.where(preact > 0, grad_out, jnp.zeros_like(grad_out))
    block = lax.all_gather(masked, "col", axis=0, tiled=True)
    row_count = block.shape[0] // 128
    row_flat = block.reshape(row_count, 128 * width)
    slots = tiles.shape[2]
    tile_stack = tiles.reshape(slots, 128, 128)
    row_index = tile_rows.reshape(slots)
    col_index = tile_cols.reshape(slots)
    count = live_counts.reshape(())
    col_tiles = lax.axis_size("row") * grad_out.shape[0] // 128
    group = math.gcd(slots, 32)
    offsets = jnp.arange(group, dtype=jnp.int32)
    row_ids = jnp.arange(row_count, dtype=jnp.int32)
    col_ids = jnp.arange(col_tiles, dtype=jnp.int32)

    def add_group(step, accum):
        start = step * group
        tile_blk = lax.dynamic_slice_in_dim(tile_stack, start, group, 0)
        rows_now = lax.dynamic_slice_in_dim(row_index, start, group, 0)
        cols_now = lax.dynamic_slice_in_dim(col_index, start, group, 0) - 0
        pick = (rows_now[:, None] == row_ids[None, :]).astype(jnp.bfloat16)
        gathered = jnp.dot(pick, row_flat, preferred_element_type=jnp.float32).astype(jnp.bfloat16)
        gathered = gathered.reshape(group, 128, width)
        prod = jnp.einsum("kab,kaf->kbf", tile_blk, gathered, preferred_element_type=jnp.float32)
        upper = prod.astype(jnp.bfloat16)
        lower = (prod - upper.astype(jnp.float32)).astype(jnp.bfloat16)
        keep = start + offsets < count
        place = ((cols_now[None, :] == col_ids[:, None]) & keep[None, :]).astype(jnp.bfloat16)
        both_place = jnp.concatenate([place, place], axis=1)
        both_vals = jnp.concatenate([upper, lower], axis=0).reshape(2 * group, 128 * width)
        return accum + jnp.dot(both_place, both_vals, preferred_element_type=jnp.float32)

    accum = jnp.zeros((col_tiles, 128 * width), jnp.float32)
    accum = lax.fori_loop(0, slots // group, add_group, accum)
    partial_value = accum.reshape(col_tiles * 128, width)
    summed = lax.psum_scatter(
        partial_value.astype(jnp.bfloat16), "row", scatter_dimension=0, tiled=True
    )
    grad_features = lax.dot_general(
        summed, weight, (((1,), (1,)), ((), ())), preferred_element_type=jnp.float32
    ).astype(jnp.bfloat16)
    weight_term = lax.dot_general(
        features, summed, (((0,), (0,)), ((), ())), preferred_element_type=jnp.float32
    )
    grad_weight = lax.psum(weight_term, ("row", "col"))
    return (grad_features, grad_weight)


def solution(mesh):
    in_specs = (
        P(("row", "col"), None),
        P(("row", "col"), None),
        P(("col", "row"), None),
        P(),
        P("row", "col", None, None, None),
        P("row", "col", None),
        P("row", "col", None),
        P("row", "col"),
    )
    out_specs = (P(("col", "row"), None), P())
    return jax.shard_map(body, mesh=mesh, in_specs=in_specs, out_specs=out_specs, check_vma=False)
```

profile of v0, /device:TPU:1, one launch (start us, length us, event | category | flops | bytes accessed | tf_op | source)
XLA Modules:
  0.0 803.8 jit_solution(6973166508205975980)
XLA Ops:
  7.2 2.7 compare_select_fusion
  10.1 14.5 %copy.12 = bf16[1,1,320,128,128]{3,4,2,1,0:T(8,128)(2,1)} copy(bf16[1,1,320,128,128]{4,3,2,1,0:T(8,128)(2,1)} %param.14) | data formatting | bytes 20971520 | tf_op args[4]
  24.6 80.9 %all-gather.2.cloned.1.call-done = bf16[16384,256]{1,0:T(8,128)(2,1)} async-done(((bf16[2048,256]{1,0:T(8,128)(2,1)}), bf16[16384,256]{1,0:T(8,128)(2,1)}) %all-gather.2.cloned.1.call-update) | async-done | bytes 8388624 | tf_op jit(solution)/shard_map/all_gather | solution.py:11
  105.4 13.4 %reshape.49 = bf16[128,32768]{1,0:T(8,128)(2,1)} reshape(bf16[16384,256]{1,0:T(8,128)(2,1)} %all-gather.2.cloned.1.call-done) | data formatting | bytes 16777216 | tf_op jit(solution)/shard_map/reshape | solution.py:13
  118.9 342.9 %while.14 = (s32[]{:T(128)}, f32[256,32768]{1,0:T(8,128)}, s32[320]{0:T(512)S(1)}, s32[]{:T(128)}, bf16[320,128,128]{1,2,0:T(8,128)(2,1)}, /*index=5*/s32[320]{0...) while((s32[]{:T(128)}, f32[256,32768]{1,0:T(8,128)}, ...), condition=%wide.region_1.2_spmd.clone, body=%wide.region_0.1_spmd.clone.sunk | while | flops 1634766848 | bytes 110117888 | solution.py:43
  119.8 4.6 convolution_convert_fusion.3
  124.9 1.9 subtract_convert_fusion.2
  127.3 2.6 copy.19
  129.8 12.4 %convolution_add_fusion.2 = f32[256,32768]{1,0:T(8,128)} fusion(bf16[64,32768]{1,0:T(8,128)(2,1)S(1)} %bitcast.29, f32[256,32768]{1,0:T(8,128)} %get-tuple-element.281, pred[]{:T(512)S(6)} %compare.3, pred[256,32]{0,1:T(32,128)(4,1)S(1)} %fusion.34), kind=kOutput, calls=%fused_computation.3.clone.1 | convolution fusion | flops 1090535424 | bytes 71311360 | tf_op jit(solution)/shard_map/while/body/eval_jaxpr/dot_general | solution.py:40
  143.2 4.6 convolution_convert_fusion.3
  148.3 1.9 subtract_convert_fusion.2
  150.6 2.6 copy.19
  153.2 24.6 %convolution_add_fusion.2 = f32[256,32768]{1,0:T(8,128)} fusion(bf16[64,32768]{1,0:T(8,128)(2,1)S(1)} %bitcast.29, f32[256,32768]{1,0:T(8,128)} %get-tuple-element.281, pred[]{:T(512)S(6)} %compare.3, pred[256,32]{0,1:T(32,128)(4,1)S(1)} %fusion.34), kind=kOutput, calls=%fused_computation.3.clone.1 | convolution fusion | flops 1090535424 | bytes 71311360 | tf_op jit(solution)/shard_map/while/body/eval_jaxpr/dot_general | solution.py:40
  178.7 4.6 convolution_convert_fusion.3
  183.8 1.9 subtract_convert_fusion.2
  186.1 2.6 copy.19
  188.7 24.6 %convolution_add_fusion.2 = f32[256,32768]{1,0:T(8,128)} fusion(bf16[64,32768]{1,0:T(8,128)(2,1)S(1)} %bitcast.29, f32[256,32768]{1,0:T(8,128)} %get-tuple-element.281, pred[]{:T(512)S(6)} %compare.3, pred[256,32]{0,1:T(32,128)(4,1)S(1)} %fusion.34), kind=kOutput, calls=%fused_computation.3.clone.1 | convolution fusion | flops 1090535424 | bytes 71311360 | tf_op jit(solution)/shard_map/while/body/eval_jaxpr/dot_general | solution.py:40
  214.2 4.6 convolution_convert_fusion.3
  219.3 1.9 subtract_convert_fusion.2
  221.6 2.6 copy.19
  224.2 24.6 %convolution_add_fusion.2 = f32[256,32768]{1,0:T(8,128)} fusion(bf16[64,32768]{1,0:T(8,128)(2,1)S(1)} %bitcast.29, f32[256,32768]{1,0:T(8,128)} %get-tuple-element.281, pred[]{:T(512)S(6)} %compare.3, pred[256,32]{0,1:T(32,128)(4,1)S(1)} %fusion.34), kind=kOutput, calls=%fused_computation.3.clone.1 | convolution fusion | flops 1090535424 | bytes 71311360 | tf_op jit(solution)/shard_map/while/body/eval_jaxpr/dot_general | solution.py:40
  249.7 4.6 convolution_convert_fusion.3
  254.8 1.9 subtract_convert_fusion.2
  257.1 2.6 copy.19
  259.7 24.6 %convolution_add_fusion.2 = f32[256,32768]{1,0:T(8,128)} fusion(bf16[64,32768]{1,0:T(8,128)(2,1)S(1)} %bitcast.29, f32[256,32768]{1,0:T(8,128)} %get-tuple-element.281, pred[]{:T(512)S(6)} %compare.3, pred[256,32]{0,1:T(32,128)(4,1)S(1)} %fusion.34), kind=kOutput, calls=%fused_computation.3.clone.1 | convolution fusion | flops 1090535424 | bytes 71311360 | tf_op jit(solution)/shard_map/while/body/eval_jaxpr/dot_general | solution.py:40
  285.2 4.6 convolution_convert_fusion.3
  290.3 1.9 subtract_convert_fusion.2
  292.6 2.6 copy.19
  295.2 24.6 %convolution_add_fusion.2 = f32[256,32768]{1,0:T(8,128)} fusion(bf16[64,32768]{1,0:T(8,128)(2,1)S(1)} %bitcast.29, f32[256,32768]{1,0:T(8,128)} %get-tuple-element.281, pred[]{:T(512)S(6)} %compare.3, pred[256,32]{0,1:T(32,128)(4,1)S(1)} %fusion.34), kind=kOutput, calls=%fused_computation.3.clone.1 | convolution fusion | flops 1090535424 | bytes 71311360 | tf_op jit(solution)/shard_map/while/body/eval_jaxpr/dot_general | solution.py:40
  320.7 4.6 convolution_convert_fusion.3
  325.8 1.9 subtract_convert_fusion.2
  328.1 2.6 copy.19
  330.7 24.6 %convolution_add_fusion.2 = f32[256,32768]{1,0:T(8,128)} fusion(bf16[64,32768]{1,0:T(8,128)(2,1)S(1)} %bitcast.29, f32[256,32768]{1,0:T(8,128)} %get-tuple-element.281, pred[]{:T(512)S(6)} %compare.3, pred[256,32]{0,1:T(32,128)(4,1)S(1)} %fusion.34), kind=kOutput, calls=%fused_computation.3.clone.1 | convolution fusion | flops 1090535424 | bytes 71311360 | tf_op jit(solution)/shard_map/while/body/eval_jaxpr/dot_general | solution.py:40
  356.2 4.6 convolution_convert_fusion.3
  363.6 2.6 copy.19
  366.2 24.6 %convolution_add_fusion.2 = f32[256,32768]{1,0:T(8,128)} fusion(bf16[64,32768]{1,0:T(8,128)(2,1)S(1)} %bitcast.29, f32[256,32768]{1,0:T(8,128)} %get-tuple-element.281, pred[]{:T(512)S(6)} %compare.3, pred[256,32]{0,1:T(32,128)(4,1)S(1)} %fusion.34), kind=kOutput, calls=%fused_computation.3.clone.1 | convolution fusion | flops 1090535424 | bytes 71311360 | tf_op jit(solution)/shard_map/while/body/eval_jaxpr/dot_general | solution.py:40
  391.7 4.6 convolution_convert_fusion.3
  399.2 2.6 copy.19
  401.7 24.6 %convolution_add_fusion.2 = f32[256,32768]{1,0:T(8,128)} fusion(bf16[64,32768]{1,0:T(8,128)(2,1)S(1)} %bitcast.29, f32[256,32768]{1,0:T(8,128)} %get-tuple-element.281, pred[]{:T(512)S(6)} %compare.3, pred[256,32]{0,1:T(32,128)(4,1)S(1)} %fusion.34), kind=kOutput, calls=%fused_computation.3.clone.1 | convolution fusion | flops 1090535424 | bytes 71311360 | tf_op jit(solution)/shard_map/while/body/eval_jaxpr/dot_general | solution.py:40
  427.2 4.6 convolution_convert_fusion.3
  434.7 2.6 copy.19
  437.2 24.6 %convolution_add_fusion.2 = f32[256,32768]{1,0:T(8,128)} fusion(bf16[64,32768]{1,0:T(8,128)(2,1)S(1)} %bitcast.29, f32[256,32768]{1,0:T(8,128)} %get-tuple-element.281, pred[]{:T(512)S(6)} %compare.3, pred[256,32]{0,1:T(32,128)(4,1)S(1)} %fusion.34), kind=kOutput, calls=%fused_computation.3.clone.1 | convolution fusion | flops 1090535424 | bytes 71311360 | tf_op jit(solution)/shard_map/while/body/eval_jaxpr/dot_general | solution.py:40
  461.8 17.1 %convert_element_type.45 = bf16[256,32768]{1,0:T(8,128)(2,1)} convert(f32[256,32768]{1,0:T(8,128)} %get-tuple-element.171) | non-fusion elementwise | flops 8388608 | bytes 50331648 | tf_op jit(solution)/shard_map/convert_element_type | solution.py:46
  478.9 25.6 %convert_element_type.46 = bf16[32768,256]{1,0:T(8,128)(2,1)} reshape(bf16[256,32768]{1,0:T(8,128)(2,1)} %convert_element_type.45) | data formatting | bytes 33554432 | tf_op jit(solution)/shard_map/convert_element_type | solution.py:46
  504.6 145.1 %reduce-scatter.2.cloned.1.call-done = bf16[2048,256]{1,0:T(8,128)(2,1)} async-done(((bf16[32768,256]{1,0:T(8,128)(2,1)}), bf16[2048,256]{1,0:T(8,128)(2,1)}) %reduce-scatter.2.cloned.1.call-update) | async-done | bytes 1048592 | tf_op jit(solution)/shard_map/reduce_scatter | solution.py:45
  649.7 2.4 convolution_bitcast_fusion
  652.1 2.7 convolution_convert_fusion.1
  654.8 140.8 %all-reduce.2.cloned.1.call-done = f32[256,256]{0,1:T(8,128)} async-done(((f32[256,256]{0,1:T(8,128)}), f32[256,256]{0,1:T(8,128)}) %all-reduce.2.cloned.1.call-update) | async-done | bytes 262160 | tf_op jit(solution)/shard_map/psum | solution.py:54
  (81 shorter events, 25.2 us)
Async XLA Ops:
  7.2 642.5 %copy-start = (bf16[2048,256]{1,0:T(8,128)(2,1)S(1)}, bf16[2048,256]{1,0:T(8,128)(2,1)}, u32[]{:S(2)}) copy-start(bf16[2048,256]{1,0:T(8,128)(2,1)} %param.12) | copy-start | bytes 3145732
  7.2 2.9 copy-start.2
  7.2 2.9 copy-start.3
  7.2 98.2 %all-gather.2.cloned.1.call-start = ((), (), s32[]{:S(2)}) async-start(), calls=%async_computation.1 | async-start | bytes 9437184 | tf_op jit(solution)/shard_map/all_gather | solution.py:11
  10.0 639.7 %reduce-scatter.2.cloned.1.call-start = ((), (), s32[]{:S(2)}) async-start(), calls=%async_computation.2 | async-start | bytes 17825792 | tf_op jit(solution)/shard_map/reduce_scatter | solution.py:45
  504.5 147.6 %copy-start.1 = (bf16[256,256]{1,0:T(8,128)(2,1)S(1)}, bf16[256,256]{1,0:T(8,128)(2,1)}, u32[]{:S(2)}) copy-start(bf16[256,256]{1,0:T(8,128)(2,1)} %param.13) | copy-start | bytes 393220
  504.6 291.0 %all-reduce.2.cloned.1.call-start = ((), (), s32[]{:S(2)}) async-start(), calls=%async_computation.3 | async-start | bytes 524288 | tf_op jit(solution)/shard_map/psum | solution.py:54
Sparse Core Ops, SparseCore 0:
  10.3 95.1 all-gather.1
  504.7 144.9 reduce-scatter.1
  655.7 139.7 all-reduce.1
where the time goes:
time: 806 us; the launch traced here: 804 us
  waiting for transfers between devices  367 us (46%)
  matrix products  304 us (38%)
  local copies, waits for them, and re-layouts  87.5 us (11%)
  other arithmetic  30.8 us (4%)
  between operations  13.8 us (2%)
    dot_general x10, matrix products, add_group(): jnp.dot(both_place, both_vals, preferred_element_type=jnp.float32)  234 us
    reduce_scatter x1, waiting for transfers between devices, body(): lax.psum_scatter(partial_value.astype(jnp.bfloat16), 'row', scatter_dimen...  145 us
    psum x1, waiting for transfers between devices, body(): grad_weight = lax.psum(weight_term, ('row', 'col'))  141 us
    all_gather x1, waiting for transfers between devices, body(): block = lax.all_gather(masked, 'col', axis=0, tiled=True)  80.9 us
    dot_general x10, matrix products, add_group(): jnp.dot(pick, row_flat, preferred_element_type=jnp.float32)  46.4 us
    while x20, local copies, waits for them, and re-layouts  30.6 us
    convert_element_type x1, local copies, waits for them, and re-layouts, body(): partial_value.astype(jnp.bfloat16)  25.6 us
    dot_general x10, matrix products, add_group(): jnp.einsum('kab,kaf->kbf', tile_blk, gathered, preferred_element_type=jnp...  19.4 us
  transfers between devices with their start and end apart: 3, of which 3 were waited for; matrix products, arithmetic and copies ran while one was open for 2% of the time, Pallas kernels for 0%

commit v1 on v0

--- a/solution.py
+++ b/solution.py
@@ -51,7 +51,8 @@
     weight_term = lax.dot_general(
         features, summed, (((0,), (0,)), ((), ())), preferred_element_type=jnp.float32
     )
-    grad_weight = lax.psum(weight_term, ("row", "col"))
+    one_axis = lax.psum(weight_term, "row")
+    grad_weight = lax.psum(one_axis, "col")
     return (grad_features, grad_weight)
 
 

time: 806 us -> 876 us (1.087)
  waiting for transfers between devices: 367 us -> 432 us
    psum x1 -> x2, waiting for transfers between devices: 141 us -> 206 us  [the longest x1 137 us: body(): one_axis = lax.psum(weight_term, 'row')]
  transfers between devices with their start and end apart: 3 -> 4, of which waited for: 3 -> 4; matrix products, arithmetic and copies ran while one was open for 2% -> 2% of each run, Pallas kernels for 0% -> 0%
where the time goes in v1:
time: 876 us; the launch traced here: 869 us
  waiting for transfers between devices  432 us (49%)
  matrix products  304 us (35%)
  local copies, waits for them, and re-layouts  87.5 us (10%)
  other arithmetic  30.8 us (4%)
  between operations  13.8 us (2%)
    dot_general x10, matrix products, add_group(): jnp.dot(both_place, both_vals, preferred_element_type=jnp.float32)  234 us
    reduce_scatter x1, waiting for transfers between devices, body(): lax.psum_scatter(partial_value.astype(jnp.bfloat16), 'row', scatter_dimen...  145 us
    psum x1, waiting for transfers between devices, body(): one_axis = lax.psum(weight_term, 'row')  137 us
    all_gather x1, waiting for transfers between devices, body(): block = lax.all_gather(masked, 'col', axis=0, tiled=True)  80.9 us
    psum x1, waiting for transfers between devices, body(): grad_weight = lax.psum(one_axis, 'col')  69.7 us
    dot_general x10, matrix products, add_group(): jnp.dot(pick, row_flat, preferred_element_type=jnp.float32)  46.4 us
    while x20, local copies, waits for them, and re-layouts  30.6 us
    convert_element_type x1, local copies, waits for them, and re-layouts, body(): partial_value.astype(jnp.bfloat16)  25.6 us
  transfers between devices with their start and end apart: 4, of which 4 were waited for; matrix products, arithmetic and copies ran while one was open for 2% of the time, Pallas kernels for 0%

profile of v1, /device:TPU:1, one launch (start us, length us, event | category | flops | bytes accessed | tf_op | source)
XLA Modules:
  0.0 869.4 jit_solution(1486265573028705820)
XLA Ops:
  7.2 2.7 compare_select_fusion
  10.1 14.5 %copy.12 = bf16[1,1,320,128,128]{3,4,2,1,0:T(8,128)(2,1)} copy(bf16[1,1,320,128,128]{4,3,2,1,0:T(8,128)(2,1)} %param.14) | data formatting | bytes 20971520 | tf_op args[4]
  24.6 80.9 %all-gather.2.cloned.1.call-done = bf16[16384,256]{1,0:T(8,128)(2,1)} async-done(((bf16[2048,256]{1,0:T(8,128)(2,1)}), bf16[16384,256]{1,0:T(8,128)(2,1)}) %all-gather.2.cloned.1.call-update) | async-done | bytes 8388624 | tf_op jit(solution)/shard_map/all_gather | solution.py:11
  105.4 13.4 %reshape.49 = bf16[128,32768]{1,0:T(8,128)(2,1)} reshape(bf16[16384,256]{1,0:T(8,128)(2,1)} %all-gather.2.cloned.1.call-done) | data formatting | bytes 16777216 | tf_op jit(solution)/shard_map/reshape | solution.py:13
  118.9 342.9 %while.14 = (s32[]{:T(128)}, f32[256,32768]{1,0:T(8,128)}, s32[320]{0:T(512)S(1)}, s32[]{:T(128)}, bf16[320,128,128]{1,2,0:T(8,128)(2,1)}, /*index=5*/s32[320]{0...) while((s32[]{:T(128)}, f32[256,32768]{1,0:T(8,128)}, ...), condition=%wide.region_1.2_spmd.clone, body=%wide.region_0.1_spmd.clone.sunk | while | flops 1634766848 | bytes 110117888 | solution.py:43
  119.8 4.6 convolution_convert_fusion.3
  124.9 1.9 subtract_convert_fusion.2
  127.3 2.6 copy.19
  129.8 12.4 %convolution_add_fusion.2 = f32[256,32768]{1,0:T(8,128)} fusion(bf16[64,32768]{1,0:T(8,128)(2,1)S(1)} %bitcast.29, f32[256,32768]{1,0:T(8,128)} %get-tuple-element.281, pred[]{:T(512)S(6)} %compare.3, pred[256,32]{0,1:T(32,128)(4,1)S(1)} %fusion.34), kind=kOutput, calls=%fused_computation.3.clone.1 | convolution fusion | flops 1090535424 | bytes 71311360 | tf_op jit(solution)/shard_map/while/body/eval_jaxpr/dot_general | solution.py:40
  143.2 4.6 convolution_convert_fusion.3
  148.3 1.9 subtract_convert_fusion.2
  150.6 2.6 copy.19
  153.2 24.6 %convolution_add_fusion.2 = f32[256,32768]{1,0:T(8,128)} fusion(bf16[64,32768]{1,0:T(8,128)(2,1)S(1)} %bitcast.29, f32[256,32768]{1,0:T(8,128)} %get-tuple-element.281, pred[]{:T(512)S(6)} %compare.3, pred[256,32]{0,1:T(32,128)(4,1)S(1)} %fusion.34), kind=kOutput, calls=%fused_computation.3.clone.1 | convolution fusion | flops 1090535424 | bytes 71311360 | tf_op jit(solution)/shard_map/while/body/eval_jaxpr/dot_general | solution.py:40
  178.7 4.6 convolution_convert_fusion.3
  183.8 1.9 subtract_convert_fusion.2
  186.1 2.6 copy.19
  188.7 24.6 %convolution_add_fusion.2 = f32[256,32768]{1,0:T(8,128)} fusion(bf16[64,32768]{1,0:T(8,128)(2,1)S(1)} %bitcast.29, f32[256,32768]{1,0:T(8,128)} %get-tuple-element.281, pred[]{:T(512)S(6)} %compare.3, pred[256,32]{0,1:T(32,128)(4,1)S(1)} %fusion.34), kind=kOutput, calls=%fused_computation.3.clone.1 | convolution fusion | flops 1090535424 | bytes 71311360 | tf_op jit(solution)/shard_map/while/body/eval_jaxpr/dot_general | solution.py:40
  214.2 4.6 convolution_convert_fusion.3
  219.3 1.9 subtract_convert_fusion.2
  221.6 2.6 copy.19
  224.2 24.6 %convolution_add_fusion.2 = f32[256,32768]{1,0:T(8,128)} fusion(bf16[64,32768]{1,0:T(8,128)(2,1)S(1)} %bitcast.29, f32[256,32768]{1,0:T(8,128)} %get-tuple-element.281, pred[]{:T(512)S(6)} %compare.3, pred[256,32]{0,1:T(32,128)(4,1)S(1)} %fusion.34), kind=kOutput, calls=%fused_computation.3.clone.1 | convolution fusion | flops 1090535424 | bytes 71311360 | tf_op jit(solution)/shard_map/while/body/eval_jaxpr/dot_general | solution.py:40
  249.7 4.6 convolution_convert_fusion.3
  254.8 1.9 subtract_convert_fusion.2
  257.1 2.6 copy.19
  259.7 24.6 %convolution_add_fusion.2 = f32[256,32768]{1,0:T(8,128)} fusion(bf16[64,32768]{1,0:T(8,128)(2,1)S(1)} %bitcast.29, f32[256,32768]{1,0:T(8,128)} %get-tuple-element.281, pred[]{:T(512)S(6)} %compare.3, pred[256,32]{0,1:T(32,128)(4,1)S(1)} %fusion.34), kind=kOutput, calls=%fused_computation.3.clone.1 | convolution fusion | flops 1090535424 | bytes 71311360 | tf_op jit(solution)/shard_map/while/body/eval_jaxpr/dot_general | solution.py:40
  285.2 4.6 convolution_convert_fusion.3
  290.3 1.9 subtract_convert_fusion.2
  292.6 2.6 copy.19
  295.2 24.6 %convolution_add_fusion.2 = f32[256,32768]{1,0:T(8,128)} fusion(bf16[64,32768]{1,0:T(8,128)(2,1)S(1)} %bitcast.29, f32[256,32768]{1,0:T(8,128)} %get-tuple-element.281, pred[]{:T(512)S(6)} %compare.3, pred[256,32]{0,1:T(32,128)(4,1)S(1)} %fusion.34), kind=kOutput, calls=%fused_computation.3.clone.1 | convolution fusion | flops 1090535424 | bytes 71311360 | tf_op jit(solution)/shard_map/while/body/eval_jaxpr/dot_general | solution.py:40
  320.7 4.6 convolution_convert_fusion.3
  328.1 2.6 copy.19
  330.7 24.6 %convolution_add_fusion.2 = f32[256,32768]{1,0:T(8,128)} fusion(bf16[64,32768]{1,0:T(8,128)(2,1)S(1)} %bitcast.29, f32[256,32768]{1,0:T(8,128)} %get-tuple-element.281, pred[]{:T(512)S(6)} %compare.3, pred[256,32]{0,1:T(32,128)(4,1)S(1)} %fusion.34), kind=kOutput, calls=%fused_computation.3.clone.1 | convolution fusion | flops 1090535424 | bytes 71311360 | tf_op jit(solution)/shard_map/while/body/eval_jaxpr/dot_general | solution.py:40
  356.2 4.6 convolution_convert_fusion.3
  363.6 2.6 copy.19
  366.2 24.6 %convolution_add_fusion.2 = f32[256,32768]{1,0:T(8,128)} fusion(bf16[64,32768]{1,0:T(8,128)(2,1)S(1)} %bitcast.29, f32[256,32768]{1,0:T(8,128)} %get-tuple-element.281, pred[]{:T(512)S(6)} %compare.3, pred[256,32]{0,1:T(32,128)(4,1)S(1)} %fusion.34), kind=kOutput, calls=%fused_computation.3.clone.1 | convolution fusion | flops 1090535424 | bytes 71311360 | tf_op jit(solution)/shard_map/while/body/eval_jaxpr/dot_general | solution.py:40
  391.7 4.6 convolution_convert_fusion.3
  399.2 2.6 copy.19
  401.7 24.6 %convolution_add_fusion.2 = f32[256,32768]{1,0:T(8,128)} fusion(bf16[64,32768]{1,0:T(8,128)(2,1)S(1)} %bitcast.29, f32[256,32768]{1,0:T(8,128)} %get-tuple-element.281, pred[]{:T(512)S(6)} %compare.3, pred[256,32]{0,1:T(32,128)(4,1)S(1)} %fusion.34), kind=kOutput, calls=%fused_computation.3.clone.1 | convolution fusion | flops 1090535424 | bytes 71311360 | tf_op jit(solution)/shard_map/while/body/eval_jaxpr/dot_general | solution.py:40
  427.2 4.6 convolution_convert_fusion.3
  434.7 2.6 copy.19
  437.2 24.6 %convolution_add_fusion.2 = f32[256,32768]{1,0:T(8,128)} fusion(bf16[64,32768]{1,0:T(8,128)(2,1)S(1)} %bitcast.29, f32[256,32768]{1,0:T(8,128)} %get-tuple-element.281, pred[]{:T(512)S(6)} %compare.3, pred[256,32]{0,1:T(32,128)(4,1)S(1)} %fusion.34), kind=kOutput, calls=%fused_computation.3.clone.1 | convolution fusion | flops 1090535424 | bytes 71311360 | tf_op jit(solution)/shard_map/while/body/eval_jaxpr/dot_general | solution.py:40
  461.8 17.1 %convert_element_type.45 = bf16[256,32768]{1,0:T(8,128)(2,1)} convert(f32[256,32768]{1,0:T(8,128)} %get-tuple-element.171) | non-fusion elementwise | flops 8388608 | bytes 50331648 | tf_op jit(solution)/shard_map/convert_element_type | solution.py:46
  478.9 25.6 %convert_element_type.46 = bf16[32768,256]{1,0:T(8,128)(2,1)} reshape(bf16[256,32768]{1,0:T(8,128)(2,1)} %convert_element_type.45) | data formatting | bytes 33554432 | tf_op jit(solution)/shard_map/convert_element_type | solution.py:46
  504.6 145.1 %reduce-scatter.2.cloned.1.call-done = bf16[2048,256]{1,0:T(8,128)(2,1)} async-done(((bf16[32768,256]{1,0:T(8,128)(2,1)}), bf16[2048,256]{1,0:T(8,128)(2,1)}) %reduce-scatter.2.cloned.1.call-update) | async-done | bytes 1048592 | tf_op jit(solution)/shard_map/reduce_scatter | solution.py:45
  649.7 2.4 convolution_bitcast_fusion
  652.1 136.6 %all-reduce.3.cloned.1.call-done = f32[256,256]{0,1:T(8,128)} async-done(((f32[256,256]{0,1:T(8,128)}), f32[256,256]{0,1:T(8,128)}) %all-reduce.3.cloned.1.call-update) | async-done | bytes 262160 | tf_op jit(solution)/shard_map/psum | solution.py:54
  788.8 2.7 convolution_convert_fusion.1
  791.5 69.7 %all-reduce.5.cloned.1.call-done = f32[256,256]{0,1:T(8,128)} async-done(((f32[256,256]{0,1:T(8,128)}), f32[256,256]{0,1:T(8,128)}) %all-reduce.5.cloned.1.call-update) | async-done | bytes 262160 | tf_op jit(solution)/shard_map/psum | solution.py:55
  (84 shorter events, 27.2 us)
Async XLA Ops:
  7.2 642.5 %copy-start = (bf16[2048,256]{1,0:T(8,128)(2,1)S(1)}, bf16[2048,256]{1,0:T(8,128)(2,1)}, u32[]{:S(2)}) copy-start(bf16[2048,256]{1,0:T(8,128)(2,1)} %param.12) | copy-start | bytes 3145732
  7.2 2.9 copy-start.2
  7.2 2.9 copy-start.3
  7.2 98.2 %all-gather.2.cloned.1.call-start = ((), (), s32[]{:S(2)}) async-start(), calls=%async_computation.1 | async-start | bytes 9437184 | tf_op jit(solution)/shard_map/all_gather | solution.py:11
  10.0 639.7 %reduce-scatter.2.cloned.1.call-start = ((), (), s32[]{:S(2)}) async-start(), calls=%async_computation.2 | async-start | bytes 17825792 | tf_op jit(solution)/shard_map/reduce_scatter | solution.py:45
  504.5 284.2 %copy-start.1 = (bf16[256,256]{1,0:T(8,128)(2,1)S(1)}, bf16[256,256]{1,0:T(8,128)(2,1)}, u32[]{:S(2)}) copy-start(bf16[256,256]{1,0:T(8,128)(2,1)} %param.13) | copy-start | bytes 393220
  504.6 284.2 %all-reduce.3.cloned.1.call-start = ((), (), s32[]{:S(2)}) async-start(), calls=%async_computation.3 | async-start | bytes 524288 | tf_op jit(solution)/shard_map/psum | solution.py:54
  652.1 209.0 %all-reduce.5.cloned.1.call-start = ((), (), s32[]{:S(2)}) async-start(), calls=%async_computation.4 | async-start | bytes 524288 | tf_op jit(solution)/shard_map/psum | solution.py:55
Sparse Core Ops, SparseCore 0:
  10.3 95.1 all-gather.1
  504.7 144.9 reduce-scatter.1
  652.9 135.8 all-reduce.2
  791.1 69.9 all-reduce.4
